TPU v7x, 32 devices: a whole 2x2x4 slice. The times are simulated.
32 devices in a mesh: grp: 2 (over y), leaf: 16 (over z, x, core).
Axes of the slice: x: 2, y: 2, z: 4, core: 2. Of those that a mesh axis runs over, the one named last changes fastest.
Arguments:
- vectors: float32 [16, 32768], P(None, ('grp', 'leaf')), may hold values from -6 to 6
- points: float32 [3, 32768], P(None, ('grp', 'leaf')), may hold values from -1 to 2
- near_lists: int32 [64, 6], P(('grp', 'leaf')), may hold values from -1 to 5, as said below
- inter_lists: int32 [64, 16], P(('grp', 'leaf')), may hold values from 0 to 31, as said below
- skeleton: int32 [64, 64], P(('grp', 'leaf')), may hold values from 0 to 511, as said below
- interp: float32 [64, 64, 512], P(('grp', 'leaf')), may hold values from -0.25 to 0.25
- transfer: float32 [64, 64, 128], P(('grp', 'leaf')), may hold values from -0.125 to 0.125
- coarse_points: float32 [2, 3, 128], replicated, may hold values from 0 to 1
Outputs:
- filtered: float32 [16, 32768], P(None, ('grp', 'leaf'))
Inputs may be any that keep to these rules, and one draw needn't show every extreme that they name: `near_lists`: place w of leaf l's window is leaf (l // 2 - 1) * 2 + w. Slot 0 holds the leaf itself (2 + l % 2); the next slots hold distinct places of other leaves of the same subtree; then -1 to the end of the row. `inter_lists`: distinct leaves of the leaf's own subtree, numbered from the subtree's first leaf, none in the leaf's window. `skeleton`: distinct places within the leaf.
All inputs are finite; a program needn't handle non-finite values.
Results may differ from a plain program's by a relative error of at most 0.00013.
Values sent between devices are 32-bit elements; how exact they have to be, the bound alone decides.
No kernel may reach another device: no remote copies, remote signals or barrier semaphores. Data moves between devices by JAX's collectives and lax.ppermute only.
A program may use at most 64 MiB of HBM per device.

v0:
```python
import jax
import jax.numpy as jnp
from jax import lax
from jax.sharding import PartitionSpec as P

kappa_scale = 3.4641016151377544
centre = 0.05
half_width = 0.05
highest = lax.Precision.HIGHEST


def with_halo(x, sides, width):
    for axis, dim in sides:
        devices, length = (lax.axis_size(axis), x.shape[dim])
        up = [(i, (i + 1) % devices) for i in range(devices - 1)]
        down = [(j, i) for i, j in up]
        last = lax.slice_in_dim(x, length - width, length, axis=dim)
        initial = lax.slice_in_dim(x, 0, width, axis=dim)
        before = lax.ppermute(last, axis, up)
        after = lax.ppermute(initial, axis, down)
        x = jnp.concatenate([before, x, after], axis=dim)
    return x


def matern(source, target):
    delta_x = source[..., 0, :, None] - target[..., 0, None, :]
    delta_y = source[..., 1, :, None] - target[..., 1, None, :]
    delta_z = source[..., 2, :, None] - target[..., 2, None, :]
    scaled = kappa_scale * jnp.sqrt(delta_x * delta_x + delta_y * delta_y + delta_z * delta_z)
    return (1.0 + scaled) * jnp.exp(-scaled)


def on_device(vectors, points, near_lists, inter_lists, skeleton, interp, transfer, coarse_points):
    per_dev = near_lists.shape[0]
    slot_count = near_lists.shape[1]
    leaf_size = interp.shape[2]
    vec_count = vectors.shape[0]
    leaf_index = lax.axis_index("leaf")
    group_index = lax.axis_index("grp")
    group_count = lax.axis_size("grp")
    leaf_points = points.reshape(3, per_dev, leaf_size).transpose(1, 0, 2)
    skel_points = jnp.take_along_axis(leaf_points, skeleton[:, None, :], axis=2)
    subtree_skel = lax.all_gather(skel_points, "leaf", axis=0, tiled=True)
    own_coarse = lax.dynamic_index_in_dim(coarse_points, group_index, 0, keepdims=False)
    apart = (jnp.arange(group_count) != group_index).astype(jnp.float32)
    coupling = matern(coarse_points, own_coarse[None]) * apart[:, None, None]
    live_slots = jnp.max(jnp.sum((near_lists >= 0).astype(jnp.int32), axis=1))
    first_leaf = leaf_index * per_dev
    subtree_lists = lax.all_gather(inter_lists, "leaf", axis=0, tiled=True)
    own_ids = first_leaf + jnp.arange(per_dev, dtype=jnp.int32)
    hits = jnp.sum(
        (subtree_lists[:, :, None] == own_ids[None, None, :]).astype(jnp.float32), axis=1
    )
    push_kernel = matern(skel_points[None], subtree_skel[:, None]) * hits[:, :, None, None]

    def operate(field):
        stacked = jnp.concatenate([points, field], axis=0)
        window = with_halo(stacked, (("leaf", 1),), per_dev * leaf_size)
        window_points = window[:3].reshape(3, 3 * per_dev, leaf_size)
        window_vecs = window[3:].reshape(vec_count, 3 * per_dev, leaf_size)

        def near_slot(slot, running):
            chosen = lax.dynamic_index_in_dim(near_lists, slot, 1, keepdims=False)
            present = (chosen >= 0).astype(jnp.float32)
            safe_place = jnp.where(chosen >= 0, chosen, 0)
            source_points = jnp.take(window_points, safe_place, axis=1).transpose(1, 0, 2)
            source_vecs = jnp.take(window_vecs, safe_place, axis=1)
            kernel = matern(source_points, leaf_points)
            product = jnp.einsum("vlp,lpq->lvq", source_vecs, kernel, precision=highest)
            return running + present[:, None, None] * product

        near_part = lax.fori_loop(
            0, live_slots, near_slot, jnp.zeros((per_dev, vec_count, leaf_size), jnp.float32)
        )
        leaf_vecs = field.reshape(vec_count, per_dev, leaf_size)
        coeffs = jnp.einsum("vlp,lrp->lvr", leaf_vecs, interp, precision=highest)
        leaf_far = lax.psum_scatter(
            jnp.einsum("jvr,tjrq->tvq", coeffs, push_kernel, precision=highest),
            "leaf",
            scatter_dimension=0,
            tiled=True,
        )
        upward = jnp.einsum("lvr,lrc->vc", coeffs, transfer, precision=highest)
        subtree_total = lax.psum(upward, "leaf")
        group_coeffs = lax.all_gather(subtree_total[None], "grp", axis=0, tiled=True)
        coarse_field = jnp.einsum("avr,arq->vq", group_coeffs, coupling, precision=highest)
        downward = leaf_far + jnp.einsum("vc,lrc->lvr", coarse_field, transfer, precision=highest)
        far_part = jnp.einsum("lvr,lrp->lvp", downward, interp, precision=highest)
        combined = (near_part + far_part) / (leaf_size * slot_count)
        return combined.transpose(1, 0, 2).reshape(vec_count, per_dev * leaf_size)

    term_one = (operate(vectors) - centre * vectors) / half_width
    term_two = 2.0 * (operate(term_one) - centre * term_one) / half_width - vectors
    term_three = 2.0 * (operate(term_two) - centre * term_two) / half_width - term_one
    squares = lax.psum(jnp.sum(term_three * term_three, axis=1), ("grp", "leaf"))
    total_points = vectors.shape[1] * group_count * lax.axis_size("leaf")
    return term_three / jnp.sqrt(squares / total_points + 1e-06)[:, None]


def solution(mesh):
    placed = (
        P(None, ("grp", "leaf")),
        P(None, ("grp", "leaf")),
        P(("grp", "leaf"), None),
        P(("grp", "leaf"), None),
        P(("grp", "leaf"), None),
        P(("grp", "leaf"), None, None),
        P(("grp", "leaf"), None, None),
        P(),
    )
    return jax.shard_map(
        on_device, mesh=mesh, in_specs=placed, out_specs=P(None, ("grp", "leaf")), check_vma=False
    )
```

profile of v0, /device:TPU:10, one launch (start us, length us, event | category | flops | bytes accessed | tf_op | source)
XLA Modules:
  0.0 312.5 jit_solution(3287674258489741425)
XLA Ops:
  6.5 0.9 pad_maximum_fusion.3
  7.5 2.1 collective-permute-start.1
  9.5 2.4 collective-permute-start
  11.9 0.9 copy.61
  13.0 1.2 gather_fusion.6
  14.4 15.5 %all-gather = s32[16,2,16]{2,1,0:T(2,128)S(1)} all-gather(s32[1,2,16]{2,1,0:T(2,128)S(1)} %bitcast.260), channel_id=1, replica_groups=mesh['grp'=2,'leaf'=16] {'leaf'}, dimensions={0}, use_global_device_ids=true | all-gather | bytes 2176 | tf_op jit(solution)/shard_map/all_gather | solution.py:49
  30.1 21.1 %all_gather.15 = f32[32,3,64]{2,1,0:T(4,128)S(1)} all-gather(f32[2,3,64]{2,1,0:T(4,128)S(1)} %bitcast_select_fusion.1), channel_id=1, replica_groups=mesh['grp'=2,'leaf'=16] {'leaf'}, dimensions={0}, use_global_device_ids=true | all-gather | bytes 26112 | tf_op jit(solution)/shard_map/all_gather | solution.py:43
  51.6 3.5 %convolution_bitcast_fusion.2 = f32[32,16,64]{2,1,0:T(8,128)} fusion(f32[32,2]{1,0:T(8,128)S(1)} %copy.67, f32[32,64]{1,0:T(8,128)S(1)} %bitcast.254, f32[2,64]{1,0:T(2,128)S(1)} %bitcast.264, f32[32,64]{1,0:T(8,128)S(1)} %bitcast.257, f32[2,64]{1,0:T(2,128)S(1)} %bitcast.267, f32[32,64]{1,0:T(8,128)S(1)} %bitcast.251, f32[2,64]{1,0:T(2,128)S(1)} %bitcast.261, ...), kind=kOutput, calls=%fused_computation.145 | convolution fusion | flops 53739520 | bytes 165632 | tf_op jit(solution)/shard_map/jvr,tjrq->tvq/dot_general | solution.py:78
  56.1 24.3 %psum.28 = f32[1,16,128]{2,1,0:T(8,128)S(1)} all-reduce(f32[1,16,128]{2,1,0:T(8,128)S(1)} %convolution_bitcast_fusion.8), channel_id=1, replica_groups=mesh['grp'=2,'leaf'=16] {'leaf'}, use_global_device_ids=true, to_apply=%region_6.9 | all-reduce | flops 2048 | bytes 16384 | tf_op jit(solution)/shard_map/psum | solution.py:84
  80.4 4.4 %all_gather.17 = f32[2,16,128]{2,1,0:T(8,128)S(1)} all-gather(f32[1,16,128]{2,1,0:T(8,128)S(1)} %psum.28), channel_id=1, replica_groups=mesh['grp'=2,'leaf'=16] {'grp'}, dimensions={0}, use_global_device_ids=true | all-gather | bytes 24576 | tf_op jit(solution)/shard_map/all_gather | solution.py:85
  85.3 0.6 reduce_max.9
  86.1 28.6 %while.30 = (s32[]{:T(128)}, f32[2,16,512]{2,1,0:T(8,128)S(1)}, s32[]{:T(128)}, s32[2,6]{0,1:T(8,128)S(1)}, f32[16,6,512]{2,0,1:T(8,128)S(1)}, /*index=5*/f32[3,...) while((s32[]{:T(128)}, f32[2,16,512]{2,1,0:T(8,128)S(1)}, s32[]{:T(128)}, ...), condition=%wide.region_3.0_spmd, body=%wide.region_2.0_spmd.sunk | while | flops 107008024 | bytes 479441 | solution.py:72
  86.7 0.6 gather_fusion
  87.9 2.8 fusion.199
  91.4 0.6 gather_fusion
  92.6 2.8 fusion.199
  96.0 0.6 gather_fusion
  97.3 2.8 fusion.199
  100.7 0.6 gather_fusion
  102.0 2.8 fusion.199
  105.4 0.6 gather_fusion
  106.6 2.8 fusion.199
  110.1 0.6 gather_fusion
  111.3 2.8 fusion.199
  114.7 0.9 fusion.116
  116.0 1.9 collective-permute-start.3
  117.9 2.4 collective-permute-start.2
  120.7 3.5 %convolution_bitcast_fusion.1 = f32[32,16,64]{2,1,0:T(8,128)} fusion(f32[32,2]{1,0:T(8,128)S(1)} %copy.67, f32[32,64]{1,0:T(8,128)S(1)} %bitcast.255, f32[2,64]{1,0:T(2,128)S(1)} %bitcast.265, f32[32,64]{1,0:T(8,128)S(1)} %bitcast.258, f32[2,64]{1,0:T(2,128)S(1)} %bitcast.268, f32[32,64]{1,0:T(8,128)S(1)} %bitcast.252, f32[2,64]{1,0:T(2,128)S(1)} %bitcast.262, ...), kind=kOutput, calls=%fused_computation.144 | convolution fusion | flops 53739520 | bytes 165632 | tf_op jit(solution)/shard_map/jvr,tjrq->tvq/dot_general | solution.py:78
  124.4 26.7 %psum.29 = f32[1,16,128]{2,1,0:T(8,128)S(1)} all-reduce(f32[1,16,128]{2,1,0:T(8,128)S(1)} %convolution_bitcast_fusion.7), channel_id=1, replica_groups=mesh['grp'=2,'leaf'=16] {'leaf'}, use_global_device_ids=true, to_apply=%region_10.13 | all-reduce | flops 2048 | bytes 16384 | tf_op jit(solution)/shard_map/psum | solution.py:84
  151.2 4.4 %all_gather.18 = f32[2,16,128]{2,1,0:T(8,128)S(1)} all-gather(f32[1,16,128]{2,1,0:T(8,128)S(1)} %psum.29), channel_id=1, replica_groups=mesh['grp'=2,'leaf'=16] {'grp'}, dimensions={0}, use_global_device_ids=true | all-gather | bytes 24576 | tf_op jit(solution)/shard_map/all_gather | solution.py:85
  156.0 28.8 %while.31 = (s32[]{:T(128)}, f32[2,16,512]{2,1,0:T(8,128)S(1)}, s32[]{:T(128)}, s32[2,6]{0,1:T(8,128)S(1)}, f32[16,6,512]{2,0,1:T(8,128)S(1)}, /*index=5*/f32[3,...) while((s32[]{:T(128)}, f32[2,16,512]{2,1,0:T(8,128)S(1)}, s32[]{:T(128)}, ...), condition=%wide.region_8.11_spmd, body=%wide.region_7.10_spmd.sunk | while | flops 107008024 | bytes 479441 | solution.py:72
  156.8 0.6 gather_fusion.2
  158.1 2.8 fusion.203
  161.5 0.6 gather_fusion.2
  162.7 2.8 fusion.203
  166.2 0.6 gather_fusion.2
  167.4 2.8 fusion.203
  170.8 0.6 gather_fusion.2
  172.1 2.8 fusion.203
  175.5 0.6 gather_fusion.2
  176.8 2.8 fusion.203
  180.2 0.6 gather_fusion.2
  181.4 2.8 fusion.203
  185.3 0.9 fusion.115
  186.6 1.9 collective-permute-start.5
  188.5 2.4 collective-permute-start.4
  191.3 3.5 %convolution_bitcast_fusion = f32[32,16,64]{2,1,0:T(8,128)} fusion(f32[32,2]{1,0:T(8,128)S(1)} %copy.67, f32[32,64]{1,0:T(8,128)S(1)} %bitcast.256, f32[2,64]{1,0:T(2,128)S(1)} %bitcast.266, f32[32,64]{1,0:T(8,128)S(1)} %bitcast.259, f32[2,64]{1,0:T(2,128)S(1)} %bitcast.269, f32[32,64]{1,0:T(8,128)S(1)} %bitcast.253, f32[2,64]{1,0:T(2,128)S(1)} %bitcast.263, ...), kind=kOutput, calls=%fused_computation.143 | convolution fusion | flops 53739520 | bytes 165632 | tf_op jit(solution)/shard_map/jvr,tjrq->tvq/dot_general | solution.py:78
  195.0 28.1 %psum.30 = f32[1,16,128]{2,1,0:T(8,128)S(1)} all-reduce(f32[1,16,128]{2,1,0:T(8,128)S(1)} %convolution_bitcast_fusion.6), channel_id=1, replica_groups=mesh['grp'=2,'leaf'=16] {'leaf'}, use_global_device_ids=true, to_apply=%region_14.17 | all-reduce | flops 2048 | bytes 16384 | tf_op jit(solution)/shard_map/psum | solution.py:84
  223.1 4.4 %all_gather.19 = f32[2,16,128]{2,1,0:T(8,128)S(1)} all-gather(f32[1,16,128]{2,1,0:T(8,128)S(1)} %psum.30), channel_id=1, replica_groups=mesh['grp'=2,'leaf'=16] {'grp'}, dimensions={0}, use_global_device_ids=true | all-gather | bytes 24576 | tf_op jit(solution)/shard_map/all_gather | solution.py:85
  227.9 28.6 %while.32 = (s32[]{:T(128)}, f32[2,16,512]{2,1,0:T(8,128)S(1)}, s32[]{:T(128)}, s32[2,6]{0,1:T(8,128)S(1)}, f32[16,6,512]{2,0,1:T(8,128)S(1)}, /*index=5*/f32[3,...) while((s32[]{:T(128)}, f32[2,16,512]{2,1,0:T(8,128)S(1)}, s32[]{:T(128)}, ...), condition=%wide.region_12.15_spmd, body=%wide.region_11.14_spmd.sunk | while | flops 107008024 | bytes 479441 | solution.py:72
  228.6 0.6 gather_fusion.4
  229.8 2.8 fusion.207
  233.2 0.6 gather_fusion.4
  234.5 2.8 fusion.207
  237.9 0.6 gather_fusion.4
  239.2 2.8 fusion.207
  242.6 0.6 gather_fusion.4
  243.8 2.8 fusion.207
  248.5 2.8 fusion.207
  253.2 2.8 fusion.207
  256.6 0.7 reduce-scatter.8.cloned.1.call-done
  257.3 0.9 fusion.114
  258.7 46.5 %psum.31 = f32[16]{0:T(128)S(1)} all-reduce(f32[16]{0:T(128)S(1)} %multiply_reduce_fusion), channel_id=1, replica_groups=mesh['grp'=2,'leaf'=16] {'grp','leaf'}, use_global_device_ids=true, to_apply=%region_16.19 | all-reduce | flops 16 | bytes 128 | tf_op jit(solution)/shard_map/psum | solution.py:95
  305.2 0.7 broadcast_divide_fusion
  (212 shorter events, 19.1 us)
Async XLA Ops:
  6.5 44.8 %copy-start = (f32[2,64,512]{2,1,0:T(8,128)S(1)}, f32[2,64,512]{2,1,0:T(8,128)}, u32[]{:S(2)}) copy-start(f32[2,64,512]{2,1,0:T(8,128)} %param.23) | copy-start | bytes 786436
  6.5 6.4 %copy-start.7 = (s32[2,64]{1,0:T(2,128)S(1)}, s32[2,64]{1,0:T(2,128)}, u32[]{:S(2)}) copy-start(s32[2,64]{1,0:T(2,128)} %param.22) | copy-start | bytes 1540
  6.5 7.8 %copy-start.5 = (s32[2,16]{1,0:T(2,128)S(1)}, s32[2,16]{1,0:T(2,128)}, u32[]{:S(2)}) copy-start(s32[2,16]{1,0:T(2,128)} %param.21) | copy-start | bytes 388
  6.5 108.2 %reduce-scatter.4.cloned.1.call-start = ((), (), s32[]{:S(2)}) async-start(), calls=%async_computation.3 | async-start | bytes 278528 | tf_op jit(solution)/shard_map/reduce_scatter | solution.py:77
  7.5 43.8 %copy-start.2 = (f32[16,1024]{1,0:T(8,128)S(1)}, f32[16,1024]{1,0:T(8,128)}, u32[]{:S(2)}) copy-start(f32[16,1024]{1,0:T(8,128)} %param.18) | copy-start | bytes 196612
  7.5 78.5 %collective-permute-start.1 = (f32[19,1024]{1,0:T(8,128)S(1)}, f32[19,1024]{1,0:T(8,128)S(1)}, u32[]{:S(2)}, u32[]{:S(2)}) collective-permute-start(f32[19,1024]{1,0:T(8,128)S(1)} %pad_maximum_fusion.3), channel_id=1, source_target_pairs={{1,0},{2,1},{3,2},{4,3},{5,4},{6,5},{7,6},{8,7},{9,8},{10,9},{11,1... | collective-permute-start | bytes 233480 | tf_op jit(solution)/shard_map/ppermute | solution.py:20
  9.5 76.4 %collective-permute-start = (f32[19,1024]{1,0:T(8,128)S(1)}, f32[19,1024]{1,0:T(8,128)S(1)}, u32[]{:S(2)}, u32[]{:S(2)}) collective-permute-start(f32[19,1024]{1,0:T(8,128)S(1)} %pad_maximum_fusion.3), channel_id=1, source_target_pairs={{0,1},{1,2},{2,3},{3,4},{4,5},{5,6},{6,7},{7,8},{8,9},{9,10},{10,1... | collective-permute-start | bytes 233480 | tf_op jit(solution)/shard_map/ppermute | solution.py:19
  55.1 0.7 copy-start.6
  55.1 0.9 copy-start.1
  55.1 29.7 %copy-start.4 = (f32[2,3,128]{2,0,1:T(2,128)S(1)}, f32[2,3,128]{2,0,1:T(2,128)}, u32[]{:S(2)}) copy-start(f32[2,3,128]{2,0,1:T(2,128)} %param.25) | copy-start | bytes 9220
  55.1 30.8 %copy-start.3 = (f32[3,1024]{1,0:T(4,128)S(1)}, f32[3,1024]{1,0:T(4,128)}, u32[]{:S(2)}) copy-start(f32[3,1024]{1,0:T(4,128)} %param.19) | copy-start | bytes 36868
  55.1 130.2 %reduce-scatter.6.cloned.1.call-start = ((), (), s32[]{:S(2)}) async-start(), calls=%async_computation.4 | async-start | bytes 278528 | tf_op jit(solution)/shard_map/reduce_scatter | solution.py:77
  116.0 39.9 %collective-permute-start.3 = (f32[19,1024]{1,0:T(8,128)S(1)}, f32[19,1024]{1,0:T(8,128)S(1)}, u32[]{:S(2)}, u32[]{:S(2)}) collective-permute-start(f32[19,1024]{1,0:T(8,128)S(1)} %pad_maximum_fusion.4), channel_id=1, source_target_pairs={{1,0},{2,1},{3,2},{4,3},{5,4},{6,5},{7,6},{8,7},{9,8},{10,9},{11,1... | collective-permute-start | bytes 233480 | tf_op jit(solution)/shard_map/ppermute | solution.py:20
  117.9 38.0 %collective-permute-start.2 = (f32[19,1024]{1,0:T(8,128)S(1)}, f32[19,1024]{1,0:T(8,128)S(1)}, u32[]{:S(2)}, u32[]{:S(2)}) collective-permute-start(f32[19,1024]{1,0:T(8,128)S(1)} %pad_maximum_fusion.4), channel_id=1, source_target_pairs={{0,1},{1,2},{2,3},{3,4},{4,5},{5,6},{6,7},{7,8},{8,9},{9,10},{10,1... | collective-permute-start | bytes 233480 | tf_op jit(solution)/shard_map/ppermute | solution.py:19
  124.4 132.9 %reduce-scatter.8.cloned.1.call-start = ((), (), s32[]{:S(2)}) async-start(), calls=%async_computation.5 | async-start | bytes 278528 | tf_op jit(solution)/shard_map/reduce_scatter | solution.py:77
  186.6 41.2 %collective-permute-start.5 = (f32[19,1024]{1,0:T(8,128)S(1)}, f32[19,1024]{1,0:T(8,128)S(1)}, u32[]{:S(2)}, u32[]{:S(2)}) collective-permute-start(f32[19,1024]{1,0:T(8,128)S(1)} %pad_maximum_fusion.5), channel_id=1, source_target_pairs={{1,0},{2,1},{3,2},{4,3},{5,4},{6,5},{7,6},{8,7},{9,8},{10,9},{11,1... | collective-permute-start | bytes 233480 | tf_op jit(solution)/shard_map/ppermute | solution.py:20
  188.5 39.3 %collective-permute-start.4 = (f32[19,1024]{1,0:T(8,128)S(1)}, f32[19,1024]{1,0:T(8,128)S(1)}, u32[]{:S(2)}, u32[]{:S(2)}) collective-permute-start(f32[19,1024]{1,0:T(8,128)S(1)} %pad_maximum_fusion.5), channel_id=1, source_target_pairs={{0,1},{1,2},{2,3},{3,4},{4,5},{5,6},{6,7},{7,8},{8,9},{9,10},{10,1... | collective-permute-start | bytes 233480 | tf_op jit(solution)/shard_map/ppermute | solution.py:19
Sparse Core Ops, SparseCore 0:
  55.2 56.6 reduce-scatter.3
  124.5 60.7 reduce-scatter.5
  195.1 62.1 reduce-scatter.7
where the time goes:
time: 313 us; the launch traced here: 312 us
  blocking collectives  175 us (56%)
  matrix products  66.6 us (21%)
  local copies, waits for them, and re-layouts  24.2 us (8%)
  loops' own time  13.7 us (4%)
  between operations  13.7 us (4%)
  starting transfers between devices  13.2 us (4%)
  other arithmetic  4.5 us (1%)
    psum x3, blocking collectives, operate(): subtree_total = lax.psum(upward, 'leaf')  79.1 us
    dot_general x18, matrix products, near_slot(): product = jnp.einsum('vlp,lpq->lvq', source_vecs, kernel, precision=highest)  50 us
    psum x1, blocking collectives, on_device(): lax.psum(jnp.sum(term_three * term_three, axis=1), ('grp', 'leaf'))  46.5 us
    all_gather x1, blocking collectives, on_device(): subtree_skel = lax.all_gather(skel_points, 'leaf', axis=0, tiled=True)  21.1 us
    all_gather x1, blocking collectives, on_device(): subtree_lists = lax.all_gather(inter_lists, 'leaf', axis=0, tiled=True)  15.5 us
    another operation x3, loops' own time, operate(): lax.fori_loop(0, live_slots, near_slot, jnp.zeros((per_dev, vec_count, le...  13.7 us
    all_gather x3, blocking collectives, operate(): lax.all_gather(subtree_total[None], 'grp', axis=0, tiled=True)  13.1 us
    dot_general x3, matrix products, operate(): jnp.einsum('jvr,tjrq->tvq', coeffs, push_kernel, precision=highest)  10.4 us
  transfers between devices with their start and end apart: 9, of which 2 were waited for; matrix products, arithmetic and copies ran while one was open for 29% of the time, Pallas kernels for 0%

commit v1 on v0

--- a/solution.py
+++ b/solution.py
@@ -7,6 +7,11 @@
 centre = 0.05
 half_width = 0.05
 highest = lax.Precision.HIGHEST
+
+
+def gather_and_add(block, mesh_axis):
+    parts = lax.all_gather(block, mesh_axis)
+    return jnp.sum(parts, axis=0)
 
 
 def with_halo(x, sides, width):
@@ -92,7 +97,7 @@
     term_one = (operate(vectors) - centre * vectors) / half_width
     term_two = 2.0 * (operate(term_one) - centre * term_one) / half_width - vectors
     term_three = 2.0 * (operate(term_two) - centre * term_two) / half_width - term_one
-    squares = lax.psum(jnp.sum(term_three * term_three, axis=1), ("grp", "leaf"))
+    squares = gather_and_add(jnp.sum(term_three * term_three, axis=1), ("grp", "leaf"))
     total_points = vectors.shape[1] * group_count * lax.axis_size("leaf")
     return term_three / jnp.sqrt(squares / total_points + 1e-06)[:, None]
 

time: 313 us -> 315 us (level)
    unnamed x0 -> x1, blocking collectives: none -> 46.9 us
    psum x1 -> x0, blocking collectives: 46.5 us -> none  [on_device(): lax.psum(jnp.sum(term_three * term_three, axis=1), ('grp', 'leaf'))]
  transfers between devices with their start and end apart: 9 -> 9, of which waited for: 2 -> 2; matrix products, arithmetic and copies ran while one was open for 29% -> 28% of each run, Pallas kernels for 0% -> 0%
where the time goes in v1:
time: 315 us; the launch traced here: 314 us
  blocking collectives  176 us (56%)
  matrix products  66.6 us (21%)
  local copies, waits for them, and re-layouts  24.5 us (8%)
  loops' own time  14.7 us (5%)
  between operations  13.7 us (4%)
  starting transfers between devices  13.2 us (4%)
  other arithmetic  4.59 us (1%)
    psum x3, blocking collectives, operate(): subtree_total = lax.psum(upward, 'leaf')  79.4 us
    dot_general x18, matrix products, near_slot(): product = jnp.einsum('vlp,lpq->lvq', source_vecs, kernel, precision=highest)  50 us
    unnamed x1, blocking collectives  46.9 us
    all_gather x1, blocking collectives, on_device(): subtree_skel = lax.all_gather(skel_points, 'leaf', axis=0, tiled=True)  21.1 us
    all_gather x1, blocking collectives, on_device(): subtree_lists = lax.all_gather(inter_lists, 'leaf', axis=0, tiled=True)  15.5 us
    another operation x3, loops' own time, operate(): lax.fori_loop(0, live_slots, near_slot, jnp.zeros((per_dev, vec_count, le...  14.7 us
    all_gather x3, blocking collectives, operate(): lax.all_gather(subtree_total[None], 'grp', axis=0, tiled=True)  13.1 us
    dot_general x3, matrix products, operate(): jnp.einsum('jvr,tjrq->tvq', coeffs, push_kernel, precision=highest)  10.4 us
  transfers between devices with their start and end apart: 9, of which 2 were waited for; matrix products, arithmetic and copies ran while one was open for 28% of the time, Pallas kernels for 0%

profile of v1, /device:TPU:10, one launch (start us, length us, event | category | flops | bytes accessed | tf_op | source)
XLA Modules:
  0.0 313.9 jit_solution(5129793640773442072)
XLA Ops:
  6.5 0.9 pad_maximum_fusion.3
  7.5 2.1 collective-permute-start.1
  9.5 2.4 collective-permute-start
  11.9 0.9 copy.61
  13.0 1.2 gather_fusion.6
  14.4 15.5 %all-gather.1 = s32[16,2,16]{2,1,0:T(2,128)S(1)} all-gather(s32[1,2,16]{2,1,0:T(2,128)S(1)} %bitcast.260), channel_id=1, replica_groups=mesh['grp'=2,'leaf'=16] {'leaf'}, dimensions={0}, use_global_device_ids=true | all-gather | bytes 2176 | tf_op jit(solution)/shard_map/all_gather | solution.py:54
  30.1 21.1 %all_gather.21 = f32[32,3,64]{2,1,0:T(4,128)S(1)} all-gather(f32[2,3,64]{2,1,0:T(4,128)S(1)} %bitcast_select_fusion.1), channel_id=1, replica_groups=mesh['grp'=2,'leaf'=16] {'leaf'}, dimensions={0}, use_global_device_ids=true | all-gather | bytes 26112 | tf_op jit(solution)/shard_map/all_gather | solution.py:48
  51.6 3.5 %convolution_bitcast_fusion.2 = f32[32,16,64]{2,1,0:T(8,128)} fusion(f32[32,2]{1,0:T(8,128)S(1)} %copy.67, f32[32,64]{1,0:T(8,128)S(1)} %bitcast.254, f32[2,64]{1,0:T(2,128)S(1)} %bitcast.264, f32[32,64]{1,0:T(8,128)S(1)} %bitcast.257, f32[2,64]{1,0:T(2,128)S(1)} %bitcast.267, f32[32,64]{1,0:T(8,128)S(1)} %bitcast.251, f32[2,64]{1,0:T(2,128)S(1)} %bitcast.261, ...), kind=kOutput, calls=%fused_computation.145 | convolution fusion | flops 53739520 | bytes 165632 | tf_op jit(solution)/shard_map/jvr,tjrq->tvq/dot_general | solution.py:83
  56.1 24.3 %psum.21 = f32[1,16,128]{2,1,0:T(8,128)S(1)} all-reduce(f32[1,16,128]{2,1,0:T(8,128)S(1)} %convolution_bitcast_fusion.8), channel_id=1, replica_groups=mesh['grp'=2,'leaf'=16] {'leaf'}, use_global_device_ids=true, to_apply=%region_6.9 | all-reduce | flops 2048 | bytes 16384 | tf_op jit(solution)/shard_map/psum | solution.py:89
  80.4 4.4 %all_gather.23 = f32[2,16,128]{2,1,0:T(8,128)S(1)} all-gather(f32[1,16,128]{2,1,0:T(8,128)S(1)} %psum.21), channel_id=1, replica_groups=mesh['grp'=2,'leaf'=16] {'grp'}, dimensions={0}, use_global_device_ids=true | all-gather | bytes 24576 | tf_op jit(solution)/shard_map/all_gather | solution.py:90
  85.3 0.7 reduce_max.9
  86.1 29.0 %while.30 = (s32[]{:T(128)}, f32[2,16,512]{2,1,0:T(8,128)S(1)}, s32[]{:T(128)}, s32[2,6]{0,1:T(8,128)S(1)}, f32[16,6,512]{2,0,1:T(8,128)S(1)}, /*index=5*/f32[3,...) while((s32[]{:T(128)}, f32[2,16,512]{2,1,0:T(8,128)S(1)}, s32[]{:T(128)}, ...), condition=%wide.region_3.0_spmd, body=%wide.region_2.0_spmd.sunk | while | flops 107008024 | bytes 479441 | solution.py:77
  86.8 0.6 gather_fusion
  88.0 2.8 fusion.199
  91.5 0.6 gather_fusion
  92.8 2.8 fusion.199
  96.2 0.6 gather_fusion
  97.5 2.8 fusion.199
  101.0 0.6 gather_fusion
  102.2 2.8 fusion.199
  105.7 0.6 gather_fusion
  107.0 2.8 fusion.199
  110.4 0.6 gather_fusion
  111.7 2.8 fusion.199
  115.1 0.9 fusion.116
  116.4 1.9 collective-permute-start.3
  118.4 2.4 collective-permute-start.2
  121.1 3.5 %convolution_bitcast_fusion.1 = f32[32,16,64]{2,1,0:T(8,128)} fusion(f32[32,2]{1,0:T(8,128)S(1)} %copy.67, f32[32,64]{1,0:T(8,128)S(1)} %bitcast.255, f32[2,64]{1,0:T(2,128)S(1)} %bitcast.265, f32[32,64]{1,0:T(8,128)S(1)} %bitcast.258, f32[2,64]{1,0:T(2,128)S(1)} %bitcast.268, f32[32,64]{1,0:T(8,128)S(1)} %bitcast.252, f32[2,64]{1,0:T(2,128)S(1)} %bitcast.262, ...), kind=kOutput, calls=%fused_computation.144 | convolution fusion | flops 53739520 | bytes 165632 | tf_op jit(solution)/shard_map/jvr,tjrq->tvq/dot_general | solution.py:83
  124.9 26.7 %psum.22 = f32[1,16,128]{2,1,0:T(8,128)S(1)} all-reduce(f32[1,16,128]{2,1,0:T(8,128)S(1)} %convolution_bitcast_fusion.7), channel_id=1, replica_groups=mesh['grp'=2,'leaf'=16] {'leaf'}, use_global_device_ids=true, to_apply=%region_10.13 | all-reduce | flops 2048 | bytes 16384 | tf_op jit(solution)/shard_map/psum | solution.py:89
  151.6 4.4 %all_gather.24 = f32[2,16,128]{2,1,0:T(8,128)S(1)} all-gather(f32[1,16,128]{2,1,0:T(8,128)S(1)} %psum.22), channel_id=1, replica_groups=mesh['grp'=2,'leaf'=16] {'grp'}, dimensions={0}, use_global_device_ids=true | all-gather | bytes 24576 | tf_op jit(solution)/shard_map/all_gather | solution.py:90
  156.4 29.2 %while.31 = (s32[]{:T(128)}, f32[2,16,512]{2,1,0:T(8,128)S(1)}, s32[]{:T(128)}, s32[2,6]{0,1:T(8,128)S(1)}, f32[16,6,512]{2,0,1:T(8,128)S(1)}, /*index=5*/f32[3,...) while((s32[]{:T(128)}, f32[2,16,512]{2,1,0:T(8,128)S(1)}, s32[]{:T(128)}, ...), condition=%wide.region_8.11_spmd, body=%wide.region_7.10_spmd.sunk | while | flops 107008024 | bytes 479441 | solution.py:77
  157.3 0.6 gather_fusion.2
  158.6 2.8 fusion.203
  162.0 0.6 gather_fusion.2
  163.3 2.8 fusion.203
  166.8 0.6 gather_fusion.2
  168.0 2.8 fusion.203
  171.5 0.6 gather_fusion.2
  172.7 2.8 fusion.203
  176.2 0.6 gather_fusion.2
  177.5 2.8 fusion.203
  180.9 0.6 gather_fusion.2
  182.2 2.8 fusion.203
  185.7 0.9 fusion.115
  187.0 1.9 collective-permute-start.5
  189.0 2.4 collective-permute-start.4
  191.7 3.5 %convolution_bitcast_fusion = f32[32,16,64]{2,1,0:T(8,128)} fusion(f32[32,2]{1,0:T(8,128)S(1)} %copy.67, f32[32,64]{1,0:T(8,128)S(1)} %bitcast.256, f32[2,64]{1,0:T(2,128)S(1)} %bitcast.266, f32[32,64]{1,0:T(8,128)S(1)} %bitcast.259, f32[2,64]{1,0:T(2,128)S(1)} %bitcast.269, f32[32,64]{1,0:T(8,128)S(1)} %bitcast.253, f32[2,64]{1,0:T(2,128)S(1)} %bitcast.263, ...), kind=kOutput, calls=%fused_computation.143 | convolution fusion | flops 53739520 | bytes 165632 | tf_op jit(solution)/shard_map/jvr,tjrq->tvq/dot_general | solution.py:83
  195.4 28.5 %psum.23 = f32[1,16,128]{2,1,0:T(8,128)S(1)} all-reduce(f32[1,16,128]{2,1,0:T(8,128)S(1)} %convolution_bitcast_fusion.6), channel_id=1, replica_groups=mesh['grp'=2,'leaf'=16] {'leaf'}, use_global_device_ids=true, to_apply=%region_14.17 | all-reduce | flops 2048 | bytes 16384 | tf_op jit(solution)/shard_map/psum | solution.py:89
  223.9 4.4 %all_gather.25 = f32[2,16,128]{2,1,0:T(8,128)S(1)} all-gather(f32[1,16,128]{2,1,0:T(8,128)S(1)} %psum.23), channel_id=1, replica_groups=mesh['grp'=2,'leaf'=16] {'grp'}, dimensions={0}, use_global_device_ids=true | all-gather | bytes 24576 | tf_op jit(solution)/shard_map/all_gather | solution.py:90
  228.7 29.0 %while.32 = (s32[]{:T(128)}, f32[2,16,512]{2,1,0:T(8,128)S(1)}, s32[]{:T(128)}, s32[2,6]{0,1:T(8,128)S(1)}, f32[16,6,512]{2,0,1:T(8,128)S(1)}, /*index=5*/f32[3,...) while((s32[]{:T(128)}, f32[2,16,512]{2,1,0:T(8,128)S(1)}, s32[]{:T(128)}, ...), condition=%wide.region_12.15_spmd, body=%wide.region_11.14_spmd.sunk | while | flops 107008024 | bytes 479441 | solution.py:77
  229.4 0.6 gather_fusion.4
  230.6 2.8 fusion.207
  234.1 0.6 gather_fusion.4
  235.4 2.8 fusion.207
  238.9 0.6 gather_fusion.4
  240.1 2.8 fusion.207
  243.6 0.6 gather_fusion.4
  244.8 2.8 fusion.207
  248.3 0.6 gather_fusion.4
  249.6 2.8 fusion.207
  254.3 2.8 fusion.207
  258.1 0.9 fusion.114
  259.7 46.9 %all-reduce = f32[512]{0:T(512)S(1)} all-reduce(f32[512]{0:T(512)S(1)} %dynamic-update-slice), channel_id=2, replica_groups=mesh['grp'=2,'leaf'=16] {'grp','leaf'}, use_global_device_ids=true, to_apply=%add | all-reduce | flops 512 | bytes 4096
  306.7 0.7 broadcast_divide_fusion
  (216 shorter events, 18.9 us)
Async XLA Ops:
  6.5 44.8 %copy-start = (f32[2,64,512]{2,1,0:T(8,128)S(1)}, f32[2,64,512]{2,1,0:T(8,128)}, u32[]{:S(2)}) copy-start(f32[2,64,512]{2,1,0:T(8,128)} %param.23) | copy-start | bytes 786436
  6.5 6.4 %copy-start.7 = (s32[2,64]{1,0:T(2,128)S(1)}, s32[2,64]{1,0:T(2,128)}, u32[]{:S(2)}) copy-start(s32[2,64]{1,0:T(2,128)} %param.22) | copy-start | bytes 1540
  6.5 7.8 %copy-start.5 = (s32[2,16]{1,0:T(2,128)S(1)}, s32[2,16]{1,0:T(2,128)}, u32[]{:S(2)}) copy-start(s32[2,16]{1,0:T(2,128)} %param.21) | copy-start | bytes 388
  6.5 108.6 %reduce-scatter.4.cloned.1.call-start = ((), (), s32[]{:S(2)}) async-start(), calls=%async_computation.3 | async-start | bytes 278528 | tf_op jit(solution)/shard_map/reduce_scatter | solution.py:82
  7.5 43.8 %copy-start.2 = (f32[16,1024]{1,0:T(8,128)S(1)}, f32[16,1024]{1,0:T(8,128)}, u32[]{:S(2)}) copy-start(f32[16,1024]{1,0:T(8,128)} %param.18) | copy-start | bytes 196612
  7.5 78.5 %collective-permute-start.1 = (f32[19,1024]{1,0:T(8,128)S(1)}, f32[19,1024]{1,0:T(8,128)S(1)}, u32[]{:S(2)}, u32[]{:S(2)}) collective-permute-start(f32[19,1024]{1,0:T(8,128)S(1)} %pad_maximum_fusion.3), channel_id=1, source_target_pairs={{1,0},{2,1},{3,2},{4,3},{5,4},{6,5},{7,6},{8,7},{9,8},{10,9},{11,1... | collective-permute-start | bytes 233480 | tf_op jit(solution)/shard_map/ppermute | solution.py:25
  9.5 76.5 %collective-permute-start = (f32[19,1024]{1,0:T(8,128)S(1)}, f32[19,1024]{1,0:T(8,128)S(1)}, u32[]{:S(2)}, u32[]{:S(2)}) collective-permute-start(f32[19,1024]{1,0:T(8,128)S(1)} %pad_maximum_fusion.3), channel_id=1, source_target_pairs={{0,1},{1,2},{2,3},{3,4},{4,5},{5,6},{6,7},{7,8},{8,9},{9,10},{10,1... | collective-permute-start | bytes 233480 | tf_op jit(solution)/shard_map/ppermute | solution.py:24
  55.1 0.7 copy-start.6
  55.1 0.9 copy-start.1
  55.1 29.7 %copy-start.4 = (f32[2,3,128]{2,0,1:T(2,128)S(1)}, f32[2,3,128]{2,0,1:T(2,128)}, u32[]{:S(2)}) copy-start(f32[2,3,128]{2,0,1:T(2,128)} %param.25) | copy-start | bytes 9220
  55.1 30.9 %copy-start.3 = (f32[3,1024]{1,0:T(4,128)S(1)}, f32[3,1024]{1,0:T(4,128)}, u32[]{:S(2)}) copy-start(f32[3,1024]{1,0:T(4,128)} %param.19) | copy-start | bytes 36868
  55.1 130.6 %reduce-scatter.6.cloned.1.call-start = ((), (), s32[]{:S(2)}) async-start(), calls=%async_computation.4 | async-start | bytes 278528 | tf_op jit(solution)/shard_map/reduce_scatter | solution.py:82
  116.4 39.9 %collective-permute-start.3 = (f32[19,1024]{1,0:T(8,128)S(1)}, f32[19,1024]{1,0:T(8,128)S(1)}, u32[]{:S(2)}, u32[]{:S(2)}) collective-permute-start(f32[19,1024]{1,0:T(8,128)S(1)} %pad_maximum_fusion.4), channel_id=1, source_target_pairs={{1,0},{2,1},{3,2},{4,3},{5,4},{6,5},{7,6},{8,7},{9,8},{10,9},{11,1... | collective-permute-start | bytes 233480 | tf_op jit(solution)/shard_map/ppermute | solution.py:25
  118.4 38.0 %collective-permute-start.2 = (f32[19,1024]{1,0:T(8,128)S(1)}, f32[19,1024]{1,0:T(8,128)S(1)}, u32[]{:S(2)}, u32[]{:S(2)}) collective-permute-start(f32[19,1024]{1,0:T(8,128)S(1)} %pad_maximum_fusion.4), channel_id=1, source_target_pairs={{0,1},{1,2},{2,3},{3,4},{4,5},{5,6},{6,7},{7,8},{8,9},{9,10},{10,1... | collective-permute-start | bytes 233480 | tf_op jit(solution)/shard_map/ppermute | solution.py:24
  124.8 133.3 %reduce-scatter.8.cloned.1.call-start = ((), (), s32[]{:S(2)}) async-start(), calls=%async_computation.5 | async-start | bytes 278528 | tf_op jit(solution)/shard_map/reduce_scatter | solution.py:82
  187.0 41.6 %collective-permute-start.5 = (f32[19,1024]{1,0:T(8,128)S(1)}, f32[19,1024]{1,0:T(8,128)S(1)}, u32[]{:S(2)}, u32[]{:S(2)}) collective-permute-start(f32[19,1024]{1,0:T(8,128)S(1)} %pad_maximum_fusion.5), channel_id=1, source_target_pairs={{1,0},{2,1},{3,2},{4,3},{5,4},{6,5},{7,6},{8,7},{9,8},{10,9},{11,1... | collective-permute-start | bytes 233480 | tf_op jit(solution)/shard_map/ppermute | solution.py:25
  189.0 39.6 %collective-permute-start.4 = (f32[19,1024]{1,0:T(8,128)S(1)}, f32[19,1024]{1,0:T(8,128)S(1)}, u32[]{:S(2)}, u32[]{:S(2)}) collective-permute-start(f32[19,1024]{1,0:T(8,128)S(1)} %pad_maximum_fusion.5), channel_id=1, source_target_pairs={{0,1},{1,2},{2,3},{3,4},{4,5},{5,6},{6,7},{7,8},{8,9},{9,10},{10,1... | collective-permute-start | bytes 233480 | tf_op jit(solution)/shard_map/ppermute | solution.py:24
Sparse Core Ops, SparseCore 0:
  55.2 56.6 reduce-scatter.3
  124.9 60.7 reduce-scatter.5
  195.5 62.5 reduce-scatter.7
